TPU v7x, 256 devices: a whole 4x4x8 slice. The times are simulated.
256 devices in a mesh: param: 16 (over z, core), ex: 16 (over x, y).
Axes of the slice: x: 4, y: 4, z: 8, core: 2. Of those that a mesh axis runs over, the one named last changes fastest.
Arguments:
- query_acts: bfloat16 [16, 256, 16, 4096], P(None, 'ex', None, 'param'), may hold values from -6 to 6
- query_grads: bfloat16 [16, 256, 16, 4096], P(None, 'ex', None, 'param'), may hold values from -6 to 6
- train_acts: bfloat16 [16, 512, 16, 4096], P(None, 'ex', None, 'param'), as said below
- train_grads: bfloat16 [16, 512, 16, 4096], P(None, 'ex', None, 'param'), as said below
- input_projection: bfloat16 [4096, 128], P('param'), as said below
- proj_out: bfloat16 [4096, 64], P('param'), as said below
- query_clusters: int32 [16, 256], P('param'), may hold values from 0 to 127
- train_clusters: int32 [16, 512], P(None, 'ex'), may hold values from 0 to 127
- pair_mask: int32 [128, 128], replicated, may hold values 0 or 1
Outputs:
- scores: float32 [16, 256, 16, 512], P('param', None, None, 'ex')
- cluster_scores: float32 [16, 256, 128], P('param', 'ex')
Inputs may be any that keep to these rules, and one draw needn't show every extreme that they name: `train_acts`: token features whose scales differ from token to token and from example to example. `train_grads`: token gradients whose scales differ from example to example. `input_projection`: random projection columns of differing scales. `proj_out`: random projection columns of differing scales.
All inputs are finite; a program needn't handle non-finite values.
Results may differ from a plain program's by a relative error of at most 0.022.
The roundings to bfloat16 on the way count: a program that leaves them out, or rounds other values in their place, can miss the bound.
Values may be sent and summed in bfloat16 or wider, within the bound.
A program may use at most 128 MiB of HBM per device.

v0:
```python
import math
import jax
import jax.numpy as jnp
from jax import lax
from jax.sharding import PartitionSpec as P


def inverse_of(gram, count):
    mean = gram / count
    size = gram.shape[0]
    damping = 0.1 * jnp.trace(mean) / size
    identity = jnp.eye(size, dtype=gram.dtype)
    factor = jnp.linalg.cholesky(mean + damping * identity)
    return jax.scipy.linalg.cho_solve((factor, True), identity)


def form_grads(part_out, part_in):
    examples = part_out.shape[0]
    grad = jnp.einsum("tkr,tks->trs", part_out, part_in, preferred_element_type=jnp.float32)
    return grad.reshape(examples, -1).astype(jnp.bfloat16)


def shards(
    query_acts,
    query_grads,
    train_acts,
    train_grads,
    input_projection,
    proj_out,
    query_clusters,
    train_clusters,
    pair_mask,
):
    group_batches = train_acts.shape[0]
    query_rows = query_acts.shape[1]
    train_rows = train_acts.shape[1]
    tokens = train_acts.shape[2]
    width_in = input_projection.shape[1]
    width_out = proj_out.shape[1]
    clusters = pair_mask.shape[0]
    pieces = []
    for acts, grads in ((query_acts, query_grads), (train_acts, train_grads)):
        lead = acts.shape[:3]
        flat_acts = acts.reshape(-1, acts.shape[3])
        flat_grads = grads.reshape(-1, grads.shape[3])
        joined = jnp.concatenate(
            [
                jnp.dot(flat_acts, input_projection, preferred_element_type=jnp.float32),
                jnp.dot(flat_grads, proj_out, preferred_element_type=jnp.float32),
            ],
            axis=1,
        )
        pieces.append(joined.reshape(lead + (width_in + width_out,)))
    projected = lax.psum_scatter(
        jnp.concatenate(pieces, axis=1), "param", scatter_dimension=0, tiled=True
    ).astype(jnp.bfloat16)
    factors = projected[0]
    query_in = factors[:query_rows, :, :width_in]
    query_output_side = factors[:query_rows, :, width_in:]
    train_in = factors[query_rows:, :, :width_in]
    train_out = factors[query_rows:, :, width_in:]
    flat_in = train_in.reshape(-1, width_in)
    flat_out = train_out.reshape(-1, width_out)
    gram_in = jnp.dot(flat_in.T, flat_in, preferred_element_type=jnp.float32)
    gram_out = jnp.dot(flat_out.T, flat_out, preferred_element_type=jnp.float32)
    gram_in, gram_out = lax.psum((gram_in, gram_out), ("param", "ex"))
    total_train = group_batches * train_rows * lax.axis_size("ex")
    count = float(total_train * tokens)
    inv_in = inverse_of(gram_in, count)
    inv_out = inverse_of(gram_out, count)
    preconditioned_input = jnp.dot(
        query_in.reshape(-1, width_in).astype(jnp.float32), inv_in, precision=lax.Precision.HIGHEST
    ).reshape(query_rows, tokens, width_in)
    preconditioned_output = jnp.dot(
        query_output_side.reshape(-1, width_out).astype(jnp.float32),
        inv_out,
        precision=lax.Precision.HIGHEST,
    ).reshape(query_rows, tokens, width_out)
    query_before_preconditioning = jnp.einsum(
        "bui,bux->bix", preconditioned_output, preconditioned_input, precision=lax.Precision.HIGHEST
    )
    query_before_preconditioning = query_before_preconditioning.reshape(query_rows, -1).astype(
        jnp.bfloat16
    )
    trains = lax.all_gather(form_grads(train_out, train_in), "param", axis=0, tiled=True)
    cluster_ids = jnp.arange(clusters, dtype=jnp.int32)
    train_onehot = train_clusters.reshape(-1)[:, None] == cluster_ids[None, :]
    train_side = train_onehot.astype(jnp.bfloat16)
    mask_values = pair_mask.astype(jnp.bfloat16)
    scale = 1.0 / (tokens * math.sqrt(width_in * width_out))
    contract = (((1,), (1,)), ((), ()))
    ids = query_clusters[0]
    query_onehot = (ids[:, None] == cluster_ids[None, :]).astype(jnp.bfloat16)
    picked = jnp.dot(query_onehot, mask_values, preferred_element_type=jnp.float32).astype(
        jnp.bfloat16
    )
    allowed = lax.dot_general(picked, train_side, contract, preferred_element_type=jnp.float32)
    raw = lax.dot_general(
        lax.all_gather(query_before_preconditioning, "ex", axis=0, tiled=True),
        trains,
        contract,
        preferred_element_type=jnp.float32,
    )
    scores = raw * scale * allowed
    partial_value = jnp.dot(
        scores, train_onehot.astype(jnp.float32), precision=lax.Precision.HIGHEST
    ) * math.sqrt(clusters / total_train)
    summed = lax.psum_scatter(
        partial_value.astype(jnp.bfloat16), "ex", scatter_dimension=0, tiled=True
    ).astype(jnp.float32)
    all_queries = scores.shape[0]
    return (
        scores.reshape(1, all_queries, group_batches, train_rows),
        summed.reshape(1, summed.shape[0], clusters),
    )


def solution(mesh):
    return jax.shard_map(
        shards,
        mesh=mesh,
        in_specs=(
            P(None, "ex", None, "param"),
            P(None, "ex", None, "param"),
            P(None, "ex", None, "param"),
            P(None, "ex", None, "param"),
            P("param", None),
            P("param", None),
            P("param", None),
            P(None, "ex"),
            P(),
        ),
        out_specs=(P("param", None, None, "ex"), P("param", "ex", None)),
        check_vma=False,
    )
```

profile of v0, /device:TPU:2, one launch (start us, length us, event | category | flops | bytes accessed | tf_op | source)
XLA Modules:
  0.0 642.3 jit_solution(12987489176357474776)
XLA Ops:
  7.2 3.8 fusion.27
  11.1 1.4 fusion.28
  12.5 3.1 pad_maximum_fusion.1
  15.6 8.4 %copy.28 = f32[8192,192]{1,0:T(8,128)} copy(f32[8192,192]{0,1:T(8,128)} %pad_maximum_fusion.1) | data formatting | bytes 12582912 | tf_op jit(solution)/shard_map/concatenate | solution.py:46
  24.1 13.1 %copy.30 = f32[16,32,16,192]{3,1,2,0:T(8,128)} copy(f32[16,32,16,192]{3,2,1,0:T(8,128)} %bitcast.70) | data formatting | bytes 12582912 | tf_op jit(solution)/shard_map/reshape | solution.py:53
  37.2 0.8 fusion.25
  39.5 2.0 pad_maximum_fusion.2
  41.4 5.1 copy.27
  46.6 7.4 %copy.29 = f32[16,16,16,192]{3,1,2,0:T(8,128)} copy(f32[16,16,16,192]{3,2,1,0:T(8,128)} %bitcast.71) | data formatting | bytes 6291456 | tf_op jit(solution)/shard_map/reshape | solution.py:53
  54.0 11.0 %pad_maximum_fusion = f32[16,48,16,192]{3,1,2,0:T(8,128)} fusion(f32[16,32,16,192]{3,1,2,0:T(8,128)} %copy.30, f32[16,16,16,192]{3,1,2,0:T(8,128)} %copy.29), kind=kLoop, calls=%fused_computation | loop fusion | flops 2359296 | bytes 18874368 | tf_op jit(solution)/shard_map/concatenate | solution.py:55
  65.1 82.4 %reduce-scatter.2.cloned.1.call-done = f32[1,48,16,192]{3,1,2,0:T(8,128)} async-done(((f32[16,48,16,192]{3,1,2,0:T(8,128)}), f32[1,48,16,192]{3,1,2,0:T(8,128)}) %reduce-scatter.2.cloned.1.call-update) | async-done | bytes 589840 | tf_op jit(solution)/shard_map/reduce_scatter | solution.py:54
  147.4 1.2 convert_bitcast_fusion
  148.6 0.9 convolution_bitcast_fusion.1
  149.8 75.2 %psum.14 = f32[64,64]{1,0:T(8,128)S(1)} all-reduce(f32[64,64]{1,0:T(8,128)S(1)} %convolution_bitcast_fusion.3), channel_id=1, replica_groups=mesh['param'=16,'ex'=16] {'param','ex'}, use_global_device_ids=true, to_apply=%region_1.0 | all-reduce | flops 4096 | bytes 32768 | tf_op jit(solution)/shard_map/psum | solution.py:66
  226.4 5.8 cholesky.33
  233.6 4.9 custom-call.20
  239.1 155.0 %all-reduce.4.cloned.1.call-done = f32[128,128]{1,0:T(8,128)} async-done(((f32[128,128]{1,0:T(8,128)}), f32[128,128]{1,0:T(8,128)}) %all-reduce.4.cloned.1.call-update) | async-done | bytes 65552 | tf_op jit(solution)/shard_map/psum | solution.py:66
  394.1 1.5 select_reduce_fusion.1
  396.3 0.9 select_add_fusion
  397.2 0.9 fusion.9
  398.1 11.7 %cholesky.68 = f32[128,128]{1,0:T(8,128)S(1)} custom-call(f32[128,128]{1,0:T(8,128)S(1)} %fusion.9), custom_call_target="Cholesky" | custom-call | tf_op jit(solution)/shard_map/jit(cholesky)/cholesky | solution.py:13
  411.1 9.8 %custom-call.21 = f32[1,128,128]{1,2,0:T(8,128)S(1)} custom-call(f32[1,128,128]{2,1,0:T(8,128)S(1)} %fusion.5), custom_call_target="InvertDiagBlocksLowerTriangular" | custom-call | tf_op jit(solution)/shard_map/jit(_cho_solve)/triangular_solve | solution.py:14
  421.6 1.0 convolution_convert_fusion.1
  422.6 0.9 copy.51
  424.0 1.1 copy.50
  425.5 51.9 %all-gather.3.cloned.1.call-done = bf16[256,8192]{1,0:T(8,128)(2,1)} async-done(((bf16[16,8192]{1,0:T(8,128)(2,1)}), bf16[256,8192]{1,0:T(8,128)(2,1)}) %all-gather.3.cloned.1.call-update) | async-done | bytes 4194320 | tf_op jit(solution)/shard_map/all_gather | solution.py:99
  477.5 57.9 %all-gather.5.cloned.1.call-done = bf16[512,8192]{1,0:T(8,128)(2,1)} async-done(((bf16[32,8192]{1,0:T(8,128)(2,1)}), bf16[512,8192]{1,0:T(8,128)(2,1)}) %all-gather.5.cloned.1.call-update) | async-done | bytes 8388624 | tf_op jit(solution)/shard_map/all_gather | solution.py:85
  535.3 7.2 %convolution_multiply_fusion.1 = f32[256,512]{1,0:T(8,128)S(1)} fusion(bf16[256,8192]{1,0:T(8,128)(2,1)} %all-gather.3.cloned.1.call-done, bf16[512,8192]{1,0:T(8,128)(2,1)} %all-gather.5.cloned.1.call-done), kind=kOutput, calls=%fused_computation.5 | convolution fusion | flops 2147614720 | bytes 13107200 | tf_op jit(solution)/shard_map/dot_general | solution.py:98
  542.9 1.1 fusion
  545.3 1.0 copy.37
  546.3 88.2 %all-reduce.6.cloned.1.call-done = bf16[256,128]{1,0:T(8,128)(2,1)} async-done(((bf16[256,128]{1,0:T(8,128)(2,1)}), bf16[256,128]{1,0:T(8,128)(2,1)}) %all-reduce.6.cloned.1.call-update) | async-done | bytes 65552
  634.5 1.3 bitcast_convert_fusion
  (57 shorter events, 8.4 us)
Async XLA Ops:
  7.2 30.0 %copy-start = (bf16[16,16,16,256]{3,2,1,0:T(8,128)(2,1)S(1)}, bf16[16,16,16,256]{3,2,1,0:T(8,128)(2,1)}, u32[]{:S(2)}) copy-start(bf16[16,16,16,256]{3,2,1,0:T(8,128)(2,1)} %param.9) | copy-start | bytes 6291460
  7.2 140.3 %reduce-scatter.2.cloned.1.call-start = ((), (), s32[]{:S(2)}) async-start(), calls=%async_computation.1 | async-start | bytes 13369344 | tf_op jit(solution)/shard_map/reduce_scatter | solution.py:54
  7.2 3.9 copy-start.2
  7.2 3.9 copy-start.5
  24.1 13.1 %copy-start.4 = (bf16[256,128]{1,0:T(8,128)(2,1)S(1)}, bf16[256,128]{1,0:T(8,128)(2,1)}, u32[]{:S(2)}) copy-start(bf16[256,128]{1,0:T(8,128)(2,1)} %param.13) | copy-start | bytes 196612
  37.1 1.6 copy-start.3
  65.0 360.5 %copy-start.7 = (s32[16,32]{1,0:T(8,128)S(1)}, s32[16,32]{1,0:T(8,128)}, u32[]{:S(2)}) copy-start(s32[16,32]{1,0:T(8,128)} %param.16) | copy-start | bytes 6148
  65.0 329.1 %all-reduce.4.cloned.1.call-start = ((), (), s32[]{:S(2)}) async-start(), calls=%async_computation.2 | async-start | bytes 131072 | tf_op jit(solution)/shard_map/psum | solution.py:66
  149.7 327.7 %all-gather.3.cloned.1.call-start = ((), (), s32[]{:S(2)}) async-start(), calls=%async_computation.3 | async-start | bytes 4456448 | tf_op jit(solution)/shard_map/all_gather | solution.py:99
  423.6 111.8 %all-gather.5.cloned.1.call-start = ((), (), s32[]{:S(2)}) async-start(), calls=%async_computation.4 | async-start | bytes 8912896 | tf_op jit(solution)/shard_map/all_gather | solution.py:85
  425.2 209.3 %all-reduce.6.cloned.1.call-start = ((), (), s32[]{:S(2)}) async-start(), calls=%async_computation.5 | async-start | bytes 131072
  425.5 117.0 %copy-start.6 = (s32[128,128]{1,0:T(8,128)S(1)}, s32[128,128]{1,0:T(8,128)}, u32[]{:S(2)}) copy-start(s32[128,128]{1,0:T(8,128)} %param.17) | copy-start | bytes 196612
  425.5 117.0 %copy-start.8 = (s32[1,256]{1,0:T(1,128)S(1)}, s32[1,256]{1,0:T(1,128)}, u32[]{:S(2)}) copy-start(s32[1,256]{1,0:T(1,128)} %param.15) | copy-start | bytes 3076
  425.5 118.5 %copy-start.9 = (u32[256]{0:T(256)S(1)}, u32[256]{0:T(256)}, u32[]{:S(2)}) copy-start(u32[256]{0:T(256)} %constant.124) | copy-start | bytes 3076
  535.3 100.4 %copy-start.1 = (bf16[16,16,16,256]{3,2,1,0:T(8,128)(2,1)S(1)}, bf16[16,16,16,256]{3,2,1,0:T(8,128)(2,1)}, u32[]{:S(2)}) copy-start(bf16[16,16,16,256]{3,2,1,0:T(8,128)(2,1)} %param.9) | copy-start | bytes 6291460
Sparse Core Ops, SparseCore 0:
  65.1 82.2 reduce-scatter.1
  153.5 240.5 all-reduce.3
  423.7 53.7 all-gather.2
  479.7 55.5 all-gather.4
  544.2 90.2 all-reduce.5
where the time goes:
time: 643 us; the launch traced here: 642 us
  waiting for transfers between devices  436 us (68%)
  blocking collectives  75.2 us (12%)
  other arithmetic  57.3 us (9%)
  local copies, waits for them, and re-layouts  38.8 us (6%)
  matrix products  19.1 us (3%)
  between operations  16 us (2%)
    psum x1, waiting for transfers between devices, shards(): gram_in, gram_out = lax.psum((gram_in, gram_out), ('param', 'ex'))  155 us
    unnamed x6, waiting for transfers between devices  88.3 us
    reduce_scatter x1, waiting for transfers between devices, shards(): lax.psum_scatter(jnp.concatenate(pieces, axis=1), 'param', scatter_dimens...  82.4 us
    psum x1, blocking collectives, shards(): gram_in, gram_out = lax.psum((gram_in, gram_out), ('param', 'ex'))  75.2 us
    all_gather x1, waiting for transfers between devices, shards(): lax.all_gather(form_grads(train_out, train_in), 'param', axis=0, tiled=True)  57.9 us
    all_gather x1, waiting for transfers between devices, shards(): lax.all_gather(query_before_preconditioning, 'ex', axis=0, tiled=True)  51.9 us
    reshape x2, local copies, waits for them, and re-layouts, shards(): pieces.append(joined.reshape(lead + (width_in + width_out,)))  20.5 us
    another operation x6, other arithmetic, inverse_of(): factor = jnp.linalg.cholesky(mean + damping * identity)  18.9 us
  transfers between devices with their start and end apart: 5, of which 5 were waited for; matrix products, arithmetic and copies ran while one was open for 3% of the time, Pallas kernels for 0%

commit v1 on v0

--- a/solution.py
+++ b/solution.py
@@ -82,7 +82,12 @@
     query_before_preconditioning = query_before_preconditioning.reshape(query_rows, -1).astype(
         jnp.bfloat16
     )
-    trains = lax.all_gather(form_grads(train_out, train_in), "param", axis=0, tiled=True)
+    trains = jnp.concatenate(
+        lax.all_to_all(
+            jnp.stack([form_grads(train_out, train_in)] * lax.axis_size("param")), "param", 0, 0
+        ),
+        axis=0,
+    )
     cluster_ids = jnp.arange(clusters, dtype=jnp.int32)
     train_onehot = train_clusters.reshape(-1)[:, None] == cluster_ids[None, :]
     train_side = train_onehot.astype(jnp.bfloat16)

time: 643 us -> 676 us (1.051)
  blocking collectives: 75.2 us -> 228 us
  waiting for transfers between devices: 436 us -> 307 us
    psum x1, blocking collectives: 75.2 us -> 228 us  [shards(): gram_in, gram_out = lax.psum((gram_in, gram_out), ('param', 'ex'))]
    psum x1, waiting for transfers between devices: 155 us -> 81.3 us  [shards(): gram_in, gram_out = lax.psum((gram_in, gram_out), ('param', 'ex'))]
    all_gather x1 -> x0, waiting for transfers between devices: 57.9 us -> none  [shards(): lax.all_gather(form_grads(train_out, train_in), 'param', axis=0, tiled=True)]
    unnamed x6 -> x5, waiting for transfers between devices: 88.3 us -> 89.4 us
  transfers between devices with their start and end apart: 5 -> 5, of which waited for: 5 -> 4; matrix products, arithmetic and copies ran while one was open for 3% -> 7% of each run, Pallas kernels for 0% -> 0%
where the time goes in v1:
time: 676 us; the launch traced here: 675 us
  waiting for transfers between devices  307 us (45%)
  blocking collectives  228 us (34%)
  other arithmetic  57.3 us (8%)
  local copies, waits for them, and re-layouts  42.2 us (6%)
  matrix products  19.1 us (3%)
  between operations  16 us (2%)
    psum x1, blocking collectives, shards(): gram_in, gram_out = lax.psum((gram_in, gram_out), ('param', 'ex'))  228 us
    unnamed x5, waiting for transfers between devices  89.4 us
    reduce_scatter x1, waiting for transfers between devices, shards(): lax.psum_scatter(jnp.concatenate(pieces, axis=1), 'param', scatter_dimens...  82.4 us
    psum x1, waiting for transfers between devices, shards(): gram_in, gram_out = lax.psum((gram_in, gram_out), ('param', 'ex'))  81.3 us
    all_gather x1, waiting for transfers between devices, shards(): lax.all_gather(query_before_preconditioning, 'ex', axis=0, tiled=True)  53.5 us
    reshape x2, local copies, waits for them, and re-layouts, shards(): pieces.append(joined.reshape(lead + (width_in + width_out,)))  20.5 us
    another operation x6, other arithmetic, inverse_of(): factor = jnp.linalg.cholesky(mean + damping * identity)  18.9 us
    another operation x4, other arithmetic, inverse_of(): return jax.scipy.linalg.cho_solve((factor, True), identity)  16 us
  transfers between devices with their start and end apart: 5, of which 4 were waited for; matrix products, arithmetic and copies ran while one was open for 7% of the time, Pallas kernels for 0%

profile of v1, /device:TPU:2, one launch (start us, length us, event | category | flops | bytes accessed | tf_op | source)
XLA Modules:
  0.0 675.4 jit_solution(18384120362491994865)
XLA Ops:
  7.2 3.8 fusion.27
  11.1 1.4 fusion.28
  12.5 3.1 pad_maximum_fusion.1
  15.6 8.4 %copy.28 = f32[8192,192]{1,0:T(8,128)} copy(f32[8192,192]{0,1:T(8,128)} %pad_maximum_fusion.1) | data formatting | bytes 12582912 | tf_op jit(solution)/shard_map/concatenate | solution.py:46
  24.1 13.1 %copy.30 = f32[16,32,16,192]{3,1,2,0:T(8,128)} copy(f32[16,32,16,192]{3,2,1,0:T(8,128)} %bitcast.71) | data formatting | bytes 12582912 | tf_op jit(solution)/shard_map/reshape | solution.py:53
  37.2 0.8 fusion.25
  39.5 2.0 pad_maximum_fusion.2
  41.4 5.1 copy.27
  46.6 7.4 %copy.29 = f32[16,16,16,192]{3,1,2,0:T(8,128)} copy(f32[16,16,16,192]{3,2,1,0:T(8,128)} %bitcast.72) | data formatting | bytes 6291456 | tf_op jit(solution)/shard_map/reshape | solution.py:53
  54.0 11.0 %pad_maximum_fusion = f32[16,48,16,192]{3,1,2,0:T(8,128)} fusion(f32[16,32,16,192]{3,1,2,0:T(8,128)} %copy.30, f32[16,16,16,192]{3,1,2,0:T(8,128)} %copy.29), kind=kLoop, calls=%fused_computation | loop fusion | flops 2359296 | bytes 18874368 | tf_op jit(solution)/shard_map/concatenate | solution.py:55
  65.0 82.4 %reduce-scatter.2.cloned.1.call-done = f32[1,48,16,192]{3,1,2,0:T(8,128)} async-done(((f32[16,48,16,192]{3,1,2,0:T(8,128)}), f32[1,48,16,192]{3,1,2,0:T(8,128)}) %reduce-scatter.2.cloned.1.call-update) | async-done | bytes 589840 | tf_op jit(solution)/shard_map/reduce_scatter | solution.py:54
  147.4 1.2 convert_bitcast_fusion
  149.4 4.2 stack.2
  153.6 5.5 all-to-all-start
  159.2 0.9 convolution_bitcast_fusion.1
  160.4 228.2 %psum.14 = f32[64,64]{1,0:T(8,128)S(1)} all-reduce(f32[64,64]{1,0:T(8,128)S(1)} %convolution_bitcast_fusion.3), channel_id=1, replica_groups=mesh['param'=16,'ex'=16] {'param','ex'}, use_global_device_ids=true, to_apply=%region_1.0 | all-reduce | flops 4096 | bytes 32768 | tf_op jit(solution)/shard_map/psum | solution.py:66
  390.0 5.8 cholesky.33
  397.1 4.9 custom-call.20
  402.7 81.3 %all-reduce.4.cloned.1.call-done = f32[128,128]{1,0:T(8,128)} async-done(((f32[128,128]{1,0:T(8,128)}), f32[128,128]{1,0:T(8,128)}) %all-reduce.4.cloned.1.call-update) | async-done | bytes 65552 | tf_op jit(solution)/shard_map/psum | solution.py:66
  483.9 1.5 select_reduce_fusion.1
  486.1 0.9 select_add_fusion
  487.0 0.9 fusion.9
  487.9 11.7 %cholesky.68 = f32[128,128]{1,0:T(8,128)S(1)} custom-call(f32[128,128]{1,0:T(8,128)S(1)} %fusion.9), custom_call_target="Cholesky" | custom-call | tf_op jit(solution)/shard_map/jit(cholesky)/cholesky | solution.py:13
  500.9 9.8 %custom-call.21 = f32[1,128,128]{1,2,0:T(8,128)S(1)} custom-call(f32[1,128,128]{2,1,0:T(8,128)S(1)} %fusion.5), custom_call_target="InvertDiagBlocksLowerTriangular" | custom-call | tf_op jit(solution)/shard_map/jit(_cho_solve)/triangular_solve | solution.py:14
  511.4 1.0 convolution_convert_fusion.1
  512.5 0.9 copy.51
  513.8 53.5 %all-gather.2.cloned.1.call-done = bf16[256,8192]{1,0:T(8,128)(2,1)} async-done(((bf16[16,8192]{1,0:T(8,128)(2,1)}), bf16[256,8192]{1,0:T(8,128)(2,1)}) %all-gather.2.cloned.1.call-update) | async-done | bytes 4194320 | tf_op jit(solution)/shard_map/all_gather | solution.py:104
  567.3 7.2 %convolution_multiply_fusion.1 = f32[256,512]{1,0:T(8,128)S(1)} fusion(bf16[256,8192]{1,0:T(8,128)(2,1)} %all-gather.2.cloned.1.call-done, bf16[512,8192]{1,0:T(8,128)(2,1)} %bitcast.17), kind=kOutput, calls=%fused_computation.5 | convolution fusion | flops 2147614720 | bytes 13107200 | tf_op jit(solution)/shard_map/dot_general | solution.py:103
  574.9 1.1 fusion
  577.3 1.0 copy.37
  578.3 89.4 %all-reduce.6.cloned.1.call-done = bf16[256,128]{1,0:T(8,128)(2,1)} async-done(((bf16[256,128]{1,0:T(8,128)(2,1)}), bf16[256,128]{1,0:T(8,128)(2,1)}) %all-reduce.6.cloned.1.call-update) | async-done | bytes 65552
  667.6 1.3 bitcast_convert_fusion
  (57 shorter events, 8.8 us)
Async XLA Ops:
  7.2 30.0 %copy-start = (bf16[16,16,16,256]{3,2,1,0:T(8,128)(2,1)S(1)}, bf16[16,16,16,256]{3,2,1,0:T(8,128)(2,1)}, u32[]{:S(2)}) copy-start(bf16[16,16,16,256]{3,2,1,0:T(8,128)(2,1)} %param.9) | copy-start | bytes 6291460
  7.2 140.3 %reduce-scatter.2.cloned.1.call-start = ((), (), s32[]{:S(2)}) async-start(), calls=%async_computation.2 | async-start | bytes 13369344 | tf_op jit(solution)/shard_map/reduce_scatter | solution.py:54
  7.2 3.9 copy-start.2
  7.2 3.9 copy-start.5
  24.1 13.1 %copy-start.4 = (bf16[256,128]{1,0:T(8,128)(2,1)S(1)}, bf16[256,128]{1,0:T(8,128)(2,1)}, u32[]{:S(2)}) copy-start(bf16[256,128]{1,0:T(8,128)(2,1)} %param.13) | copy-start | bytes 196612
  37.1 1.6 copy-start.3
  153.6 413.6 %all-to-all-start = ((bf16[16,32,8192]{2,1,0:T(8,128)(2,1)}), bf16[16,32,8192]{2,1,0:T(8,128)(2,1)}, u32[]{:S(2)}, u32[]{:S(2)}) async-start(bf16[16,32,8192]{2,1,0:T(8,128)(2,1)} %stack.2), calls=%async_computation.1 | async-start | bytes 16777216 | tf_op jit(solution)/shard_map/all_to_all | solution.py:86
  159.1 354.5 %copy-start.7 = (s32[16,32]{1,0:T(8,128)S(1)}, s32[16,32]{1,0:T(8,128)}, u32[]{:S(2)}) copy-start(s32[16,32]{1,0:T(8,128)} %param.16) | copy-start | bytes 6148
  159.1 324.8 %all-reduce.4.cloned.1.call-start = ((), (), s32[]{:S(2)}) async-start(), calls=%async_computation.3 | async-start | bytes 131072 | tf_op jit(solution)/shard_map/psum | solution.py:66
  160.1 407.2 %all-gather.2.cloned.1.call-start = ((), (), s32[]{:S(2)}) async-start(), calls=%async_computation.4 | async-start | bytes 4456448 | tf_op jit(solution)/shard_map/all_gather | solution.py:104
  513.4 154.3 %all-reduce.6.cloned.1.call-start = ((), (), s32[]{:S(2)}) async-start(), calls=%async_computation.5 | async-start | bytes 131072
  567.3 7.2 %copy-start.6 = (s32[128,128]{1,0:T(8,128)S(1)}, s32[128,128]{1,0:T(8,128)}, u32[]{:S(2)}) copy-start(s32[128,128]{1,0:T(8,128)} %param.17) | copy-start | bytes 196612
  567.3 7.2 %copy-start.8 = (s32[1,256]{1,0:T(1,128)S(1)}, s32[1,256]{1,0:T(1,128)}, u32[]{:S(2)}) copy-start(s32[1,256]{1,0:T(1,128)} %param.15) | copy-start | bytes 3076
  567.3 8.7 %copy-start.9 = (u32[256]{0:T(256)S(1)}, u32[256]{0:T(256)}, u32[]{:S(2)}) copy-start(u32[256]{0:T(256)} %constant.124) | copy-start | bytes 3076
  567.3 101.6 %copy-start.1 = (bf16[16,16,16,256]{3,2,1,0:T(8,128)(2,1)S(1)}, bf16[16,16,16,256]{3,2,1,0:T(8,128)(2,1)}, u32[]{:S(2)}) copy-start(bf16[16,16,16,256]{3,2,1,0:T(8,128)(2,1)} %param.9) | copy-start | bytes 6291460
Sparse Core Ops, SparseCore 0:
  65.1 82.2 reduce-scatter.1
  166.0 317.8 all-reduce.3
  513.5 53.7 all-gather.1
  576.1 91.4 all-reduce.5
